TPU v7x, 256 devices: a whole 4x4x8 slice. The times are simulated.
256 devices in a mesh: gx: 16 (over x, y), gy: 2 (over core), gz: 8 (over z).
Axes of the slice: x: 4, y: 4, z: 8, core: 2. Of those that a mesh axis runs over, the one named last changes fastest.
Arguments:
- field: float32 [2, 1024, 128, 1024], P(None, 'gx', 'gy', 'gz'), as said below
- start_basis: float32 [1024, 256], replicated, may hold values from -6 to 6
Outputs:
- factor: float32 [1024, 256], P('gx')
- core: float32 [2, 256, 128, 1024], P(None, 'gx', 'gy', 'gz')
Inputs may be any that keep to these rules, and one draw needn't show every extreme that they name: Real-valued field; no structure is promised.
All inputs are finite; a program needn't handle non-finite values.
Results may differ from a plain program's by a relative error of at most 0.0002.
Values sent between devices are 32-bit elements; how exact they have to be, the bound alone decides.
A program may use at most 64 MiB of HBM per device.

v0:
```python
import jax
import jax.numpy as jnp
from jax import lax
from jax.sharding import PartitionSpec as P

ITERS = 2


def orthonormal(image):
    small = jnp.dot(image.T, image, precision=lax.Precision.HIGHEST)
    lower = jnp.linalg.cholesky(small)
    return jax.scipy.linalg.solve_triangular(lower, image.T, lower=True).T


def per_device(field, start_basis):
    comps, slab, cells_y, cells_z = field.shape
    flat_field = field.reshape(comps, slab, cells_y * cells_z)
    fibers = lax.all_to_all(flat_field, "gx", split_axis=2, concat_axis=1, tiled=True)
    basis = start_basis
    local_gram = jnp.einsum("crm,csm->rs", fibers, fibers, precision=lax.Precision.HIGHEST)
    gram = lax.psum(local_gram, ("gx", "gy", "gz"))
    for step in range(ITERS):
        image = jnp.dot(gram, basis, precision=lax.Precision.HIGHEST)
        basis = orthonormal(image)
    projected = jnp.einsum("rk,crm->ckm", basis, fibers, precision=lax.Precision.HIGHEST)
    returned = lax.all_to_all(projected, "gx", split_axis=1, concat_axis=2, tiled=True)
    offset = lax.axis_index("gx") * slab
    factor = lax.dynamic_slice_in_dim(basis, offset, slab, 0)
    return (factor, returned.reshape(comps, returned.shape[1], cells_y, cells_z))


def solution(mesh):
    placed = (P(None, "gx", "gy", "gz"), P())
    return jax.shard_map(
        per_device,
        mesh=mesh,
        in_specs=placed,
        out_specs=(P("gx", None), P(None, "gx", "gy", "gz")),
        check_vma=False,
    )
```

profile of v0, /device:TPU:97, one launch (start us, length us, event | category | flops | bytes accessed | tf_op | source)
XLA Modules:
  0.0 604.0 jit_solution(12621777568615691695)
XLA Ops:
  7.2 8.4 %copy.13 = f32[2,64,64,128]{1,0,3,2:T(2,128)} copy(f32[2,64,64,128]{3,2,1,0:T(8,128)} %param.5) | data formatting | bytes 8388608 | tf_op args[0]
  15.7 15.1 %reshape.52 = f32[16,1,65536]{2,1,0:T(1,128)} reshape(f32[8192,2,64]{2,1,0:T(2,128)} %bitcast.97) | data formatting | bytes 8388608
  30.8 56.1 %all_to_all.33 = f32[16,1,65536]{2,1,0:T(1,128)} all-to-all(f32[16,1,65536]{2,1,0:T(1,128)} %reshape.52), channel_id=1, replica_groups=mesh['gx'=16,'gy'=2,'gz'=8] {'gx'}, dimensions={0} | all-to-all | bytes 8388608 | tf_op jit(solution)/shard_map/all_to_all | solution.py:18
  87.3 13.7 %reduce.8 = f32[16,65536]{1,0:T(8,128)} reduce(f32[16,1,65536]{2,1,0:T(1,128)} %all_to_all.33, f32[]{:T(128)} %broadcast.87), dimensions={1}, to_apply=%all_to_all.24.reduce_sub_computation | reduce | bytes 8388612 | tf_op jit(solution)/shard_map/all_to_all | solution.py:18
  101.0 9.7 %reshape.53 = f32[8192,2,64]{2,1,0:T(2,128)} reshape(f32[16,65536]{1,0:T(8,128)} %reduce.8) | data formatting | bytes 8388608
  110.7 12.2 %copy.26 = f32[2,64,16,512]{3,1,2,0:T(8,128)} copy(f32[2,64,16,512]{1,0,3,2:T(2,128)} %bitcast.96) | data formatting | bytes 8388608 | tf_op jit(solution)/shard_map/all_to_all | solution.py:18
  122.9 17.6 %convolution_bitcast_fusion = f32[1024,1024]{1,0:T(8,128)} fusion(f32[2,1024,512]{2,1,0:T(8,128)} %bitcast.98), kind=kOutput, calls=%fused_computation.4 | convolution fusion | flops 12884901888 | bytes 8388608 | tf_op jit(solution)/shard_map/crm,csm->rs/dot_general | solution.py:20
  140.6 270.4 %all-reduce.3.cloned.1.call-done = f32[1024,1024]{1,0:T(8,128)} async-done(((f32[1024,1024]{1,0:T(8,128)}), f32[1024,1024]{1,0:T(8,128)}) %all-reduce.3.cloned.1.call-update) | async-done | bytes 4194320 | tf_op jit(solution)/shard_map/psum | solution.py:21
  411.0 5.5 fusion.32
  416.5 1.8 fusion.33
  418.5 11.7 %cholesky.130 = f32[128,128]{1,0:T(8,128)S(1)} custom-call(f32[128,128]{1,0:T(8,128)S(1)} %cholesky.194), custom_call_target="Cholesky" | custom-call | tf_op jit(solution)/shard_map/jit(cholesky)/cholesky | solution.py:11
  430.3 9.8 %custom-call.13 = f32[1,128,128]{1,2,0:T(8,128)S(1)} custom-call(f32[1,128,128]{2,1,0:T(8,128)S(1)} %get-tuple-element.53), custom_call_target="InvertDiagBlocksLowerTriangular" | custom-call | tf_op jit(solution)/shard_map/jit(cholesky)/cholesky | solution.py:11
  440.6 11.7 %cholesky.147 = f32[128,128]{1,0:T(8,128)S(1)} custom-call(f32[128,128]{1,0:T(8,128)S(1)} %convolution_subtract_fusion.3), custom_call_target="Cholesky" | custom-call | tf_op jit(solution)/shard_map/jit(cholesky)/cholesky | solution.py:11
  467.2 3.9 while.4
  471.2 19.7 %custom-call.14 = f32[2,128,128]{1,2,0:T(8,128)S(1)} custom-call(f32[2,128,128]{2,1,0:T(8,128)S(1)} %get-tuple-element.18), custom_call_target="InvertDiagBlocksLowerTriangular" | custom-call | tf_op jit(solution)/shard_map/jit(_solve_triangular)/triangular_solve | solution.py:12
  493.2 5.3 fusion.2
  500.5 11.7 %cholesky.164 = f32[128,128]{1,0:T(8,128)S(1)} custom-call(f32[128,128]{1,0:T(8,128)S(1)} %cholesky.197), custom_call_target="Cholesky" | custom-call | tf_op jit(solution)/shard_map/jit(cholesky)/cholesky | solution.py:11
  512.3 9.8 %custom-call.15 = f32[1,128,128]{1,2,0:T(8,128)S(1)} custom-call(f32[1,128,128]{2,1,0:T(8,128)S(1)} %get-tuple-element.49), custom_call_target="InvertDiagBlocksLowerTriangular" | custom-call | tf_op jit(solution)/shard_map/jit(cholesky)/cholesky | solution.py:11
  522.6 11.7 %cholesky.181 = f32[128,128]{1,0:T(8,128)S(1)} custom-call(f32[128,128]{1,0:T(8,128)S(1)} %convolution_subtract_fusion.2), custom_call_target="Cholesky" | custom-call | tf_op jit(solution)/shard_map/jit(cholesky)/cholesky | solution.py:11
  537.2 4.0 while.5
  541.2 19.7 %custom-call.16 = f32[2,128,128]{1,2,0:T(8,128)S(1)} custom-call(f32[2,128,128]{2,1,0:T(8,128)S(1)} %get-tuple-element.19), custom_call_target="InvertDiagBlocksLowerTriangular" | custom-call | tf_op jit(solution)/shard_map/jit(_solve_triangular)/triangular_solve | solution.py:12
  563.2 5.7 convolution_bitcast_fusion.1
  570.7 4.6 all-to-all-start.1
  576.1 17.8 %all-to-all-done.1 = f32[2,256,512]{2,0,1:T(2,128)} async-done(((f32[2,256,512]{2,0,1:T(2,128)}), f32[2,256,512]{2,0,1:T(2,128)}, u32[]{:S(2)}, u32[]{:S(2)}) %all-to-all-start.1) | async-done | bytes 1048608 | tf_op jit(solution)/shard_map/all_to_all | solution.py:26
  (54 shorter events, 24.0 us)
Async XLA Ops:
  7.2 403.9 %copy-start = (f32[1024,256]{1,0:T(8,128)S(1)}, f32[1024,256]{1,0:T(8,128)}, u32[]{:S(2)}) copy-start(f32[1024,256]{1,0:T(8,128)} %param.6) | copy-start | bytes 3145732
  7.2 403.8 %all-reduce.3.cloned.1.call-start = ((), (), s32[]{:S(2)}) async-start(), calls=%async_computation.2 | async-start | bytes 8388608 | tf_op jit(solution)/shard_map/psum | solution.py:21
  570.7 23.2 %all-to-all-start.1 = ((f32[2,256,512]{2,0,1:T(2,128)}), f32[2,256,512]{2,0,1:T(2,128)}, u32[]{:S(2)}, u32[]{:S(2)}) async-start(f32[2,256,512]{2,0,1:T(2,128)} %copy.20), calls=%async_computation.1 | async-start | bytes 2097152 | tf_op jit(solution)/shard_map/all_to_all | solution.py:26
Sparse Core Ops, SparseCore 0:
  140.7 270.2 all-reduce.2
where the time goes:
time: 614 us; the launch traced here: 604 us
  waiting for transfers between devices  288 us (47%)
  other arithmetic  122 us (20%)
  local copies, waits for them, and re-layouts  59.5 us (10%)
  blocking collectives  56.1 us (9%)
  matrix products  43.3 us (7%)
  between operations  30.1 us (5%)
    psum x1, waiting for transfers between devices, per_device(): gram = lax.psum(local_gram, ('gx', 'gy', 'gz'))  270 us
    another operation x13, other arithmetic, orthonormal(): lower = jnp.linalg.cholesky(small)  68.5 us
    all_to_all x1, blocking collectives, per_device(): lax.all_to_all(flat_field, 'gx', split_axis=2, concat_axis=1, tiled=True)  56.1 us
    another operation x5, other arithmetic, orthonormal(): return jax.scipy.linalg.solve_triangular(lower, image.T, lower=True).T  39.6 us
    unnamed x6, local copies, waits for them, and re-layouts  33.9 us
    all_to_all x1, waiting for transfers between devices, per_device(): lax.all_to_all(projected, 'gx', split_axis=1, concat_axis=2, tiled=True)  17.8 us
    dot_general x1, matrix products, per_device(): jnp.einsum('crm,csm->rs', fibers, fibers, precision=lax.Precision.HIGHEST)  17.6 us
    all_to_all x1, other arithmetic, per_device(): lax.all_to_all(flat_field, 'gx', split_axis=2, concat_axis=1, tiled=True)  13.7 us
  transfers between devices with their start and end apart: 2, of which 2 were waited for; matrix products, arithmetic and copies ran while one was open for 0% of the time, Pallas kernels for 0%

commit v1 on v0

--- a/solution.py
+++ b/solution.py
@@ -4,6 +4,22 @@
 from jax.sharding import PartitionSpec as P
 
 ITERS = 2
+
+
+def test_sections(m, k_dim, inp):
+    found_now = m.shape
+    tmp = m.reshape(*found_now[:k_dim], inp, found_now[k_dim] // inp, *found_now[k_dim + 1 :])
+    return jnp.moveaxis(tmp, k_dim, 0)
+
+
+def finish_sizes_on_mesh(x_part, on_dim):
+    x_part = jnp.moveaxis(x_part, 0, on_dim)
+    current_block = x_part.shape
+    return x_part.reshape(
+        *current_block[:on_dim],
+        current_block[on_dim] * current_block[on_dim + 1],
+        *current_block[on_dim + 2 :]
+    )
 
 
 def orthonormal(image):
@@ -23,7 +39,24 @@
         image = jnp.dot(gram, basis, precision=lax.Precision.HIGHEST)
         basis = orthonormal(image)
     projected = jnp.einsum("rk,crm->ckm", basis, fibers, precision=lax.Precision.HIGHEST)
-    returned = lax.all_to_all(projected, "gx", split_axis=1, concat_axis=2, tiled=True)
+
+    def finish_pieces_all_here(patch, named_axis, body, buf):
+        earlier = lax.axis_index(named_axis)
+        plain = lax.axis_size(named_axis)
+        t1, tile_out = (plain, earlier)
+        m_next = test_sections(patch, body, t1)
+        f_now = m_next
+        dev_j = 1
+        while dev_j < t1:
+            b_now, tall = ((tile_out + dev_j) % t1, (tile_out - dev_j) % t1)
+            step_out = lax.dynamic_index_in_dim(m_next, b_now, 0)
+            back = tuple(((no, (no + dev_j) % t1) for no in range(t1)))
+            part_next = lax.ppermute(step_out, named_axis, back)
+            f_now = lax.dynamic_update_slice_in_dim(f_now, part_next, tall, axis=0)
+            dev_j += 1
+        return finish_sizes_on_mesh(f_now, buf)
+
+    returned = finish_pieces_all_here(projected, "gx", 1, 2)
     offset = lax.axis_index("gx") * slab
     factor = lax.dynamic_slice_in_dim(basis, offset, slab, 0)
     return (factor, returned.reshape(comps, returned.shape[1], cells_y, cells_z))

time: 614 us -> 612 us (level)
  the two profiles are of different devices: /device:TPU:97 before, /device:TPU:24 now
where the time goes in v1:
time: 612 us; the launch traced here: 602 us
  waiting for transfers between devices  276 us (45%)
  other arithmetic  122 us (20%)
  local copies, waits for them, and re-layouts  57 us (9%)
  blocking collectives  56.1 us (9%)
  matrix products  43.5 us (7%)
  starting transfers between devices  29 us (5%)
  between operations  18.1 us (3%)
    psum x1, waiting for transfers between devices, per_device(): gram = lax.psum(local_gram, ('gx', 'gy', 'gz'))  270 us
    another operation x13, other arithmetic, orthonormal(): lower = jnp.linalg.cholesky(small)  68.6 us
    all_to_all x1, blocking collectives, per_device(): lax.all_to_all(flat_field, 'gx', split_axis=2, concat_axis=1, tiled=True)  56.1 us
    another operation x5, other arithmetic, orthonormal(): return jax.scipy.linalg.solve_triangular(lower, image.T, lower=True).T  39.8 us
    unnamed x6, local copies, waits for them, and re-layouts  33.9 us
    ppermute x15, starting transfers between devices, finish_pieces_all_here(): part_next = lax.ppermute(step_out, named_axis, back)  28.9 us
    dot_general x1, matrix products, per_device(): jnp.einsum('crm,csm->rs', fibers, fibers, precision=lax.Precision.HIGHEST)  18.1 us
    all_to_all x1, other arithmetic, per_device(): lax.all_to_all(flat_field, 'gx', split_axis=2, concat_axis=1, tiled=True)  13.7 us
  transfers between devices with their start and end apart: 16, of which 4 were waited for; matrix products, arithmetic and copies ran while one was open for 0% of the time, Pallas kernels for 0%

profile of v1, /device:TPU:24, one launch (start us, length us, event | category | flops | bytes accessed | tf_op | source)
XLA Modules:
  0.0 602.0 jit_solution(6911518079677584891)
XLA Ops:
  7.2 8.4 %copy.13 = f32[2,64,64,128]{1,0,3,2:T(2,128)} copy(f32[2,64,64,128]{3,2,1,0:T(8,128)} %param.5) | data formatting | bytes 8388608 | tf_op args[0]
  15.7 15.1 %reshape.66 = f32[16,1,65536]{2,1,0:T(1,128)} reshape(f32[8192,2,64]{2,1,0:T(2,128)} %bitcast.128) | data formatting | bytes 8388608
  30.8 56.1 %all_to_all.18 = f32[16,1,65536]{2,1,0:T(1,128)} all-to-all(f32[16,1,65536]{2,1,0:T(1,128)} %reshape.66), channel_id=1, replica_groups=mesh['gx'=16,'gy'=2,'gz'=8] {'gx'}, dimensions={0} | all-to-all | bytes 8388608 | tf_op jit(solution)/shard_map/all_to_all | solution.py:34
  87.4 13.7 %reduce.8 = f32[16,65536]{1,0:T(8,128)} reduce(f32[16,1,65536]{2,1,0:T(1,128)} %all_to_all.18, f32[]{:T(128)} %broadcast.117), dimensions={1}, to_apply=%all_to_all.13.reduce_sub_computation | reduce | bytes 8388612 | tf_op jit(solution)/shard_map/all_to_all | solution.py:34
  101.1 9.7 %reshape.67 = f32[8192,2,64]{2,1,0:T(2,128)} reshape(f32[16,65536]{1,0:T(8,128)} %reduce.8) | data formatting | bytes 8388608
  110.7 12.2 %copy.25 = f32[2,64,16,512]{3,1,2,0:T(8,128)} copy(f32[2,64,16,512]{1,0,3,2:T(2,128)} %bitcast.127) | data formatting | bytes 8388608 | tf_op jit(solution)/shard_map/all_to_all | solution.py:34
  122.9 18.1 %convolution_bitcast_fusion = f32[1024,1024]{1,0:T(8,128)} fusion(f32[2,1024,512]{2,1,0:T(8,128)} %bitcast.129), kind=kOutput, calls=%fused_computation.4 | convolution fusion | flops 12884901888 | bytes 8388608 | tf_op jit(solution)/shard_map/crm,csm->rs/dot_general | solution.py:36
  141.6 269.7 %all-reduce.3.cloned.1.call-done = f32[1024,1024]{1,0:T(8,128)} async-done(((f32[1024,1024]{1,0:T(8,128)}), f32[1024,1024]{1,0:T(8,128)}) %all-reduce.3.cloned.1.call-update) | async-done | bytes 4194320 | tf_op jit(solution)/shard_map/psum | solution.py:37
  411.4 5.2 fusion.33
  418.6 11.7 %cholesky.130 = f32[128,128]{1,0:T(8,128)S(1)} custom-call(f32[128,128]{1,0:T(8,128)S(1)} %cholesky.194), custom_call_target="Cholesky" | custom-call | tf_op jit(solution)/shard_map/jit(cholesky)/cholesky | solution.py:27
  430.4 9.8 %custom-call.13 = f32[1,128,128]{1,2,0:T(8,128)S(1)} custom-call(f32[1,128,128]{2,1,0:T(8,128)S(1)} %get-tuple-element.68), custom_call_target="InvertDiagBlocksLowerTriangular" | custom-call | tf_op jit(solution)/shard_map/jit(cholesky)/cholesky | solution.py:27
  440.7 11.7 %cholesky.147 = f32[128,128]{1,0:T(8,128)S(1)} custom-call(f32[128,128]{1,0:T(8,128)S(1)} %convolution_subtract_fusion.3), custom_call_target="Cholesky" | custom-call | tf_op jit(solution)/shard_map/jit(cholesky)/cholesky | solution.py:27
  454.8 4.1 while.4
  458.9 19.7 %custom-call.14 = f32[2,128,128]{1,2,0:T(8,128)S(1)} custom-call(f32[2,128,128]{2,1,0:T(8,128)S(1)} %get-tuple-element.18), custom_call_target="InvertDiagBlocksLowerTriangular" | custom-call | tf_op jit(solution)/shard_map/jit(_solve_triangular)/triangular_solve | solution.py:28
  480.9 5.3 fusion.3
  488.3 11.7 %cholesky.164 = f32[128,128]{1,0:T(8,128)S(1)} custom-call(f32[128,128]{1,0:T(8,128)S(1)} %cholesky.197), custom_call_target="Cholesky" | custom-call | tf_op jit(solution)/shard_map/jit(cholesky)/cholesky | solution.py:27
  500.1 9.8 %custom-call.15 = f32[1,128,128]{1,2,0:T(8,128)S(1)} custom-call(f32[1,128,128]{2,1,0:T(8,128)S(1)} %get-tuple-element.64), custom_call_target="InvertDiagBlocksLowerTriangular" | custom-call | tf_op jit(solution)/shard_map/jit(cholesky)/cholesky | solution.py:27
  510.4 11.7 %cholesky.181 = f32[128,128]{1,0:T(8,128)S(1)} custom-call(f32[128,128]{1,0:T(8,128)S(1)} %convolution_subtract_fusion.2), custom_call_target="Cholesky" | custom-call | tf_op jit(solution)/shard_map/jit(cholesky)/cholesky | solution.py:27
  525.1 4.0 while.5
  529.2 19.7 %custom-call.16 = f32[2,128,128]{1,2,0:T(8,128)S(1)} custom-call(f32[2,128,128]{2,1,0:T(8,128)S(1)} %get-tuple-element.19), custom_call_target="InvertDiagBlocksLowerTriangular" | custom-call | tf_op jit(solution)/shard_map/jit(_solve_triangular)/triangular_solve | solution.py:28
  551.1 5.7 fusion.1
  562.7 4.2 collective-permute-start.4
  580.0 6.0 collective-permute-start.12
  588.5 4.8 collective-permute-done.13
  (97 shorter events, 43.8 us)
Async XLA Ops:
  7.2 404.2 %copy-start = (f32[1024,256]{1,0:T(8,128)S(1)}, f32[1024,256]{1,0:T(8,128)}, u32[]{:S(2)}) copy-start(f32[1024,256]{1,0:T(8,128)} %param.6) | copy-start | bytes 3145732
  7.2 404.2 %all-reduce.3.cloned.1.call-start = ((), (), s32[]{:S(2)}) async-start(), calls=%async_computation.1 | async-start | bytes 8388608 | tf_op jit(solution)/shard_map/psum | solution.py:37
  557.0 10.6 %collective-permute-start = (f32[1,2,16,512]{3,2,0,1:T(8,128)S(1)}, f32[1,2,16,512]{3,2,0,1:T(8,128)S(1)}, u32[]{:S(2)}, u32[]{:S(2)}) collective-permute-start(f32[1,2,16,512]{3,2,0,1:T(8,128)S(1)} %get-tuple-element.60), channel_id=1, source_target_pairs={{0,16},{16,32},{32,48},{48,64},{64,80},{80,96},{96,112},{112,128},... | collective-permute-start | bytes 196616 | tf_op jit(solution)/shard_map/ppermute | solution.py:54
  558.6 10.9 %collective-permute-start.1 = (f32[1,2,16,512]{3,2,0,1:T(8,128)S(1)}, f32[1,2,16,512]{3,2,0,1:T(8,128)S(1)}, u32[]{:S(2)}, u32[]{:S(2)}) collective-permute-start(f32[1,2,16,512]{3,2,0,1:T(8,128)S(1)} %get-tuple-element.59), channel_id=1, source_target_pairs={{0,32},{16,48},{32,64},{48,80},{64,96},{80,112},{96,128},{112,144}... | collective-permute-start | bytes 196616 | tf_op jit(solution)/shard_map/ppermute | solution.py:54
  560.6 9.3 %collective-permute-start.2 = (f32[1,2,16,512]{3,2,0,1:T(8,128)S(1)}, f32[1,2,16,512]{3,2,0,1:T(8,128)S(1)}, u32[]{:S(2)}, u32[]{:S(2)}) collective-permute-start(f32[1,2,16,512]{3,2,0,1:T(8,128)S(1)} %get-tuple-element.58), channel_id=1, source_target_pairs={{0,48},{16,64},{32,80},{48,96},{64,112},{80,128},{96,144},{112,160... | collective-permute-start | bytes 196616 | tf_op jit(solution)/shard_map/ppermute | solution.py:54
  561.5 11.7 %collective-permute-start.3 = (f32[1,2,16,512]{3,2,0,1:T(8,128)S(1)}, f32[1,2,16,512]{3,2,0,1:T(8,128)S(1)}, u32[]{:S(2)}, u32[]{:S(2)}) collective-permute-start(f32[1,2,16,512]{3,2,0,1:T(8,128)S(1)} %get-tuple-element.57), channel_id=1, source_target_pairs={{0,64},{16,80},{32,96},{48,112},{64,128},{80,144},{96,160},{112,17... | collective-permute-start | bytes 196616 | tf_op jit(solution)/shard_map/ppermute | solution.py:54
  562.7 12.7 %collective-permute-start.4 = (f32[1,2,16,512]{3,2,0,1:T(8,128)S(1)}, f32[1,2,16,512]{3,2,0,1:T(8,128)S(1)}, u32[]{:S(2)}, u32[]{:S(2)}) collective-permute-start(f32[1,2,16,512]{3,2,0,1:T(8,128)S(1)} %get-tuple-element.56), channel_id=1, source_target_pairs={{0,80},{16,96},{32,112},{48,128},{64,144},{80,160},{96,176},{112,1... | collective-permute-start | bytes 196616 | tf_op jit(solution)/shard_map/ppermute | solution.py:54
  567.7 11.4 %collective-permute-start.5 = (f32[1,2,16,512]{3,2,0,1:T(8,128)S(1)}, f32[1,2,16,512]{3,2,0,1:T(8,128)S(1)}, u32[]{:S(2)}, u32[]{:S(2)}) collective-permute-start(f32[1,2,16,512]{3,2,0,1:T(8,128)S(1)} %get-tuple-element.55), channel_id=1, source_target_pairs={{0,96},{16,112},{32,128},{48,144},{64,160},{80,176},{96,192},{112,... | collective-permute-start | bytes 196616 | tf_op jit(solution)/shard_map/ppermute | solution.py:54
  569.5 9.6 %collective-permute-start.6 = (f32[1,2,16,512]{3,2,0,1:T(8,128)S(1)}, f32[1,2,16,512]{3,2,0,1:T(8,128)S(1)}, u32[]{:S(2)}, u32[]{:S(2)}) collective-permute-start(f32[1,2,16,512]{3,2,0,1:T(8,128)S(1)} %get-tuple-element.54), channel_id=1, source_target_pairs={{0,112},{16,128},{32,144},{48,160},{64,176},{80,192},{96,208},{112... | collective-permute-start | bytes 196616 | tf_op jit(solution)/shard_map/ppermute | solution.py:54
  569.9 10.1 %collective-permute-start.7 = (f32[1,2,16,512]{3,2,0,1:T(8,128)S(1)}, f32[1,2,16,512]{3,2,0,1:T(8,128)S(1)}, u32[]{:S(2)}, u32[]{:S(2)}) collective-permute-start(f32[1,2,16,512]{3,2,0,1:T(8,128)S(1)} %get-tuple-element.53), channel_id=1, source_target_pairs={{0,128},{16,144},{32,160},{48,176},{64,192},{80,208},{96,224},{112... | collective-permute-start | bytes 196616 | tf_op jit(solution)/shard_map/ppermute | solution.py:54
  573.2 12.8 %collective-permute-start.8 = (f32[1,2,16,512]{3,2,0,1:T(8,128)S(1)}, f32[1,2,16,512]{3,2,0,1:T(8,128)S(1)}, u32[]{:S(2)}, u32[]{:S(2)}) collective-permute-start(f32[1,2,16,512]{3,2,0,1:T(8,128)S(1)} %get-tuple-element.52), channel_id=1, source_target_pairs={{0,144},{16,160},{32,176},{48,192},{64,208},{80,224},{96,240},{112... | collective-permute-start | bytes 196616 | tf_op jit(solution)/shard_map/ppermute | solution.py:54
  575.4 10.7 %collective-permute-start.9 = (f32[1,2,16,512]{3,2,0,1:T(8,128)S(1)}, f32[1,2,16,512]{3,2,0,1:T(8,128)S(1)}, u32[]{:S(2)}, u32[]{:S(2)}) collective-permute-start(f32[1,2,16,512]{3,2,0,1:T(8,128)S(1)} %get-tuple-element.51), channel_id=1, source_target_pairs={{0,160},{16,176},{32,192},{48,208},{64,224},{80,240},{96,0},{112,1... | collective-permute-start | bytes 196616 | tf_op jit(solution)/shard_map/ppermute | solution.py:54
  579.0 8.7 %collective-permute-start.10 = (f32[1,2,16,512]{3,2,0,1:T(8,128)S(1)}, f32[1,2,16,512]{3,2,0,1:T(8,128)S(1)}, u32[]{:S(2)}, u32[]{:S(2)}) collective-permute-start(f32[1,2,16,512]{3,2,0,1:T(8,128)S(1)} %get-tuple-element.50), channel_id=1, source_target_pairs={{0,176},{16,192},{32,208},{48,224},{64,240},{80,0},{96,16},{112,32... | collective-permute-start | bytes 196616 | tf_op jit(solution)/shard_map/ppermute | solution.py:54
  579.2 8.6 %collective-permute-start.11 = (f32[1,2,16,512]{3,2,0,1:T(8,128)S(1)}, f32[1,2,16,512]{3,2,0,1:T(8,128)S(1)}, u32[]{:S(2)}, u32[]{:S(2)}) collective-permute-start(f32[1,2,16,512]{3,2,0,1:T(8,128)S(1)} %get-tuple-element.49), channel_id=1, source_target_pairs={{0,192},{16,208},{32,224},{48,240},{64,0},{80,16},{96,32},{112,48}... | collective-permute-start | bytes 196616 | tf_op jit(solution)/shard_map/ppermute | solution.py:54
  580.0 8.5 %collective-permute-start.12 = (f32[1,2,16,512]{3,2,0,1:T(8,128)S(1)}, f32[1,2,16,512]{3,2,0,1:T(8,128)S(1)}, u32[]{:S(2)}, u32[]{:S(2)}) collective-permute-start(f32[1,2,16,512]{3,2,0,1:T(8,128)S(1)} %get-tuple-element.48), channel_id=1, source_target_pairs={{0,208},{16,224},{32,240},{48,0},{64,16},{80,32},{96,48},{112,64},... | collective-permute-start | bytes 196616 | tf_op jit(solution)/shard_map/ppermute | solution.py:54
  586.0 7.3 %collective-permute-start.13 = (f32[1,2,16,512]{3,2,0,1:T(8,128)S(1)}, f32[1,2,16,512]{3,2,0,1:T(8,128)S(1)}, u32[]{:S(2)}, u32[]{:S(2)}) collective-permute-start(f32[1,2,16,512]{3,2,0,1:T(8,128)S(1)} %get-tuple-element.47), channel_id=1, source_target_pairs={{0,224},{16,240},{32,0},{48,16},{64,32},{80,48},{96,64},{112,80},{... | collective-permute-start | bytes 196616 | tf_op jit(solution)/shard_map/ppermute | solution.py:54
  586.1 7.2 %collective-permute-start.14 = (f32[1,2,16,512]{3,2,0,1:T(8,128)S(1)}, f32[1,2,16,512]{3,2,0,1:T(8,128)S(1)}, u32[]{:S(2)}, u32[]{:S(2)}) collective-permute-start(f32[1,2,16,512]{3,2,0,1:T(8,128)S(1)} %get-tuple-element.46), channel_id=1, source_target_pairs={{0,240},{16,0},{32,16},{48,32},{64,48},{80,64},{96,80},{112,96},{1... | collective-permute-start | bytes 196616 | tf_op jit(solution)/shard_map/ppermute | solution.py:54
Sparse Core Ops, SparseCore 0:
  141.2 270.1 all-reduce.2
